TPU v7x, 512 devices: a whole 4x8x8 slice. The times are simulated.
512 devices in a mesh: blk: 16 (over z, y_lo), tan: 32 (over y_hi, x, core).
Axes of the slice: x: 4, y: 8 (y_hi: 4, y_lo: 2; y = y_hi * 2 + y_lo), z: 8, core: 2. Of those that a mesh axis runs over, the one named last changes fastest.
Arguments:
- layer_in: bfloat16 [2048, 256], P('blk'), may hold values from -6 to 6
- laplace_in: bfloat16 [2048, 256], P('blk'), may hold values from -6 to 6
- tangent_in: bfloat16 [2048, 64, 256], P('blk', 'tan'), may hold values from -1.5 to 1.5
- spin_labels: int32 [2048], P('blk'), may hold values from 0 to 1
- pair_bias: bfloat16 [2048, 2048], P('blk'), may hold values from -6 to 306
- query_weight: bfloat16 [256, 256], replicated, may hold values from -0.375 to 0.375
- key_weight: bfloat16 [256, 256], replicated, may hold values from -0.375 to 0.375
- value_weight: bfloat16 [256, 256], replicated, may hold values from -0.375 to 0.375
- out_weight: bfloat16 [256, 256], replicated, may hold values from -0.375 to 0.375
- head_gain: float32 [4], replicated, may hold values from 0.5 to 2
- spin_gain: float32 [4], replicated, may hold values from -2 to 2
Outputs:
- layer_out: bfloat16 [2048, 256], P('blk')
- tangent_out: bfloat16 [2048, 64, 256], P('blk', 'tan')
- laplacian_out: float32 [2048, 256], P('blk')
All inputs are finite; a program needn't handle non-finite values.
Results may differ from a plain program's by a relative error of at most 0.02.
Values may be sent and summed in bfloat16 or wider, within the bound.
A program may use at most 64 MiB of HBM per device.

v0:
```python
import math
import jax
import jax.numpy as jnp
from jax import lax
from jax.sharding import PartitionSpec as P


def project(rows, weight):
    return jnp.dot(rows, weight, preferred_element_type=jnp.float32).astype(jnp.bfloat16)


def project_tangent(tangent, weight):
    count, dirs, width = tangent.shape
    return project(tangent.reshape(count * dirs, width), weight).reshape(count, dirs, width)


def on_device(
    layer_in,
    laplace_in,
    tangent_in,
    spin_labels,
    pair_bias,
    query_weight,
    key_weight,
    value_weight,
    out_weight,
    head_gain,
    spin_gain,
):
    rows, width = layer_in.shape
    heads = head_gain.shape[0]
    head_size = width // heads
    dirs = tangent_in.shape[1]
    scale = 1.0 / math.sqrt(head_size)
    bias_cols = lax.all_to_all(pair_bias, "blk", split_axis=1, concat_axis=0, tiled=True)
    query = project(layer_in, query_weight).reshape(rows, heads, head_size)
    lap_query = project(laplace_in, query_weight).reshape(rows, heads, head_size)
    tan_query = project_tangent(tangent_in, query_weight).reshape(rows, dirs, heads, head_size)
    spin_query = spin_labels.astype(jnp.float32)
    spin_wire = spin_labels.astype(jnp.bfloat16)

    def attend(carry, block, first):
        top, total, numer, tan_total, tan_numer, lap_total, lap_numer, trace_total, trace_numer = (
            carry
        )
        key_b, value_b, lap_key_b, lap_value_b, tan_key_b, tan_value_b, spin_key = block
        count = key_b.shape[0]
        key_h = key_b.reshape(count, heads, head_size)
        value_h = value_b.reshape(count, heads, head_size)
        lap_key_h = lap_key_b.reshape(count, heads, head_size)
        lap_value_h = lap_value_b.reshape(count, heads, head_size)
        tan_key_h = tan_key_b.reshape(count, dirs, heads, head_size)
        tan_value_h = tan_value_b.reshape(count, dirs, heads, head_size)
        bias_rows = lax.dynamic_slice_in_dim(bias_cols, first, count, 0).astype(jnp.float32)
        spin_float = spin_key.astype(jnp.float32)
        same = (
            spin_query[:, None] * spin_float[None, :]
            + (1.0 - spin_query)[:, None] * (1.0 - spin_float)[None, :]
        )
        scores = (
            jnp.einsum("ihd,jhd->hij", query, key_h, preferred_element_type=jnp.float32) * scale
        )
        scores = (
            scores
            + head_gain[:, None, None] * bias_rows.T[None]
            + spin_gain[:, None, None] * same[None]
        )
        new_top = jnp.maximum(top, jnp.max(scores, axis=2))
        shrink = jnp.exp(top - new_top)
        shrink_rows = shrink.T[:, :, None]
        unnorm = jnp.exp(scores - new_top[:, :, None])
        weights = unnorm.astype(jnp.bfloat16)
        total = total * shrink + jnp.sum(unnorm, axis=2)
        numer = numer * shrink_rows + jnp.einsum(
            "hij,jhd->ihd", weights, value_h, preferred_element_type=jnp.float32
        )
        lap_scores = (
            jnp.einsum("ihd,jhd->hij", lap_query, key_h, preferred_element_type=jnp.float32)
            + jnp.einsum("ihd,jhd->hij", query, lap_key_h, preferred_element_type=jnp.float32)
        ) * scale
        lap_weighted = unnorm * lap_scores
        lap_total = lap_total * shrink + jnp.sum(lap_weighted, axis=2)
        lap_numer = (
            lap_numer * shrink_rows
            + jnp.einsum(
                "hij,jhd->ihd",
                lap_weighted.astype(jnp.bfloat16),
                value_h,
                preferred_element_type=jnp.float32,
            )
            + jnp.einsum("hij,jhd->ihd", weights, lap_value_h, preferred_element_type=jnp.float32)
        )
        tan_scores = (
            jnp.einsum("iahd,jhd->ahij", tan_query, key_h, preferred_element_type=jnp.float32)
            + jnp.einsum("ihd,jahd->ahij", query, tan_key_h, preferred_element_type=jnp.float32)
        ) * scale
        cross = (
            jnp.einsum("iahd,jahd->ahij", tan_query, tan_key_h, preferred_element_type=jnp.float32)
            * scale
        )
        tan_weighted = unnorm[None] * tan_scores
        tan_weights = tan_weighted.astype(jnp.bfloat16)
        tan_total = tan_total * shrink[None] + jnp.sum(tan_weighted, axis=3)
        tan_numer = (
            tan_numer * shrink_rows[:, None]
            + jnp.einsum("ahij,jhd->iahd", tan_weights, value_h, preferred_element_type=jnp.float32)
            + jnp.einsum("hij,jahd->iahd", weights, tan_value_h, preferred_element_type=jnp.float32)
        )
        second = unnorm[None] * (tan_scores * tan_scores + 2.0 * cross)
        trace_total = trace_total * shrink + jnp.sum(second, axis=(0, 3))
        trace_numer = (
            trace_numer * shrink_rows
            + jnp.einsum(
                "ahij,jhd->ihd",
                second.astype(jnp.bfloat16),
                value_h,
                preferred_element_type=jnp.float32,
            )
            + 2.0
            * jnp.einsum(
                "ahij,jahd->ihd", tan_weights, tan_value_h, preferred_element_type=jnp.float32
            )
        )
        return (
            new_top,
            total,
            numer,
            tan_total,
            tan_numer,
            lap_total,
            lap_numer,
            trace_total,
            trace_numer,
        )

    head_zeros = jnp.zeros((heads, rows), jnp.float32)
    row_zeros = jnp.zeros((rows, heads, head_size), jnp.float32)
    start_carry = (
        jnp.full((heads, rows), -1e30, jnp.float32),
        head_zeros,
        row_zeros,
        jnp.zeros((dirs, heads, rows), jnp.float32),
        jnp.zeros((rows, dirs, heads, head_size), jnp.float32),
        head_zeros,
        row_zeros,
        head_zeros,
        row_zeros,
    )
    own_keys = project(layer_in, key_weight)
    own_values = project(layer_in, value_weight)
    own_lap_keys = project(laplace_in, key_weight)
    own_lap_values = project(laplace_in, value_weight)
    own_tan_keys = project_tangent(tangent_in, key_weight)
    own_tan_values = project_tangent(tangent_in, value_weight)
    block = (
        lax.all_gather(own_keys, "blk", axis=0, tiled=True),
        lax.all_gather(own_values, "blk", axis=0, tiled=True),
        lax.all_gather(own_lap_keys, "blk", axis=0, tiled=True),
        lax.all_gather(own_lap_values, "blk", axis=0, tiled=True),
        lax.all_gather(own_tan_keys, "blk", axis=0, tiled=True),
        lax.all_gather(own_tan_values, "blk", axis=0, tiled=True),
        lax.all_gather(spin_wire, "blk", axis=0, tiled=True),
    )
    count = block[0].shape[0]
    size = 256
    parts = count // size
    stacked = tuple((piece.reshape((parts, size) + piece.shape[1:]) for piece in block))

    def step(inner, item):
        number, pieces = item
        return (attend(inner, pieces, number * size), None)

    result, _ = lax.scan(step, start_carry, (jnp.arange(parts, dtype=jnp.int32), stacked))
    top, total, numer, tan_total, tan_numer, lap_total, lap_numer, trace_total, trace_numer = result
    denom = total.T[:, :, None]
    denom_sq = denom * denom
    attn = numer / denom
    tan_denom = jnp.transpose(tan_total, (2, 0, 1))[..., None]
    attn_tan = tan_numer / denom[:, None] - numer[:, None] * tan_denom / denom_sq[:, None]
    cross_sum = jnp.sum(tan_numer * tan_denom, axis=1)
    square_sum = jnp.sum(tan_denom * tan_denom, axis=1)
    own_terms = (
        trace_numer / denom
        - numer * trace_total.T[:, :, None] / denom_sq
        - 2.0 * cross_sum / denom_sq
        + 2.0 * numer * square_sum / (denom_sq * denom)
    )
    shared = lax.psum(own_terms.reshape(rows, width).astype(jnp.bfloat16), "tan").astype(
        jnp.float32
    )
    attn_lap = (lap_numer / denom - numer * lap_total.T[:, :, None] / denom_sq).reshape(
        rows, width
    ) + shared
    layer_out = (
        jnp.dot(
            attn.reshape(rows, width).astype(jnp.bfloat16),
            out_weight,
            preferred_element_type=jnp.float32,
        )
        + layer_in.astype(jnp.float32)
    ).astype(jnp.bfloat16)
    tan_flat = attn_tan.reshape(rows * dirs, width).astype(jnp.bfloat16)
    tangent_out = jnp.dot(tan_flat, out_weight, preferred_element_type=jnp.float32).reshape(
        rows, dirs, width
    )
    tangent_out = (tangent_out + tangent_in.astype(jnp.float32)).astype(jnp.bfloat16)
    laplacian_out = jnp.dot(
        attn_lap.astype(jnp.bfloat16), out_weight, preferred_element_type=jnp.float32
    ) + laplace_in.astype(jnp.float32)
    return (layer_out, tangent_out, laplacian_out)


def solution(mesh):
    in_specs = (
        P("blk", None),
        P("blk", None),
        P("blk", "tan", None),
        P("blk"),
        P("blk", None),
        P(),
        P(),
        P(),
        P(),
        P(),
        P(),
    )
    out_specs = (P("blk", None), P("blk", "tan", None), P("blk", None))
    return jax.shard_map(
        on_device, mesh=mesh, in_specs=in_specs, out_specs=out_specs, check_vma=False
    )
```

profile of v0, /device:TPU:8, one launch (start us, length us, event | category | flops | bytes accessed | tf_op | source)
XLA Modules:
  0.0 942.7 jit_solution(8929567075966488008)
XLA Ops:
  7.2 1.8 convolution_convert_fusion.8
  9.1 1.7 convolution_convert_fusion.3
  10.9 1.7 convolution_convert_fusion.6
  12.7 1.7 convolution_convert_fusion.4
  19.4 11.8 %all-to-all-start = ((bf16[128,16,128]{2,0,1:T(8,128)(2,1)}), bf16[128,16,128]{2,0,1:T(8,128)(2,1)}, u32[]{:S(2)}, u32[]{:S(2)}) async-start(bf16[128,16,128]{2,0,1:T(8,128)(2,1)} %copy_bitcast_fusion), calls=%async_computation | async-start | bytes 1048576 | tf_op jit(solution)/shard_map/all_to_all | solution.py:35
  32.5 34.9 %all-gather = bf16[16,1,128]{2,1,0:T(2,128)(2,1)S(1)} all-gather(bf16[1,1,128]{2,1,0:T(2,128)(2,1)S(1)} %get-tuple-element.593), channel_id=1, replica_groups=mesh['blk'=16,'tan'=32] {'blk'}, dimensions={0}, use_global_device_ids=true | all-gather | bytes 4352 | tf_op jit(solution)/shard_map/all_gather | solution.py:162
  69.9 20.5 %all-gather.8.cloned.1.call-done = bf16[2048,256]{1,0:T(8,128)(2,1)} async-done(((bf16[128,256]{1,0:T(8,128)(2,1)}), bf16[2048,256]{1,0:T(8,128)(2,1)}) %all-gather.8.cloned.1.call-update) | async-done | bytes 1048592 | tf_op jit(solution)/shard_map/all_gather | solution.py:156
  90.4 74.6 %all-gather.18.cloned.1.call-done = bf16[2048,256]{1,0:T(8,128)(2,1)} async-done(((bf16[128,256]{1,0:T(8,128)(2,1)}), bf16[2048,256]{1,0:T(8,128)(2,1)}) %all-gather.18.cloned.1.call-update) | async-done | bytes 1048592 | tf_op jit(solution)/shard_map/all_gather | solution.py:159
  165.0 75.4 %all-gather.10.cloned.1.call-done = bf16[2048,256]{1,0:T(8,128)(2,1)} async-done(((bf16[128,256]{1,0:T(8,128)(2,1)}), bf16[2048,256]{1,0:T(8,128)(2,1)}) %all-gather.10.cloned.1.call-update) | async-done | bytes 1048592 | tf_op jit(solution)/shard_map/all_gather | solution.py:157
  240.4 75.2 %all-gather.16.cloned.1.call-done = bf16[2048,256]{1,0:T(8,128)(2,1)} async-done(((bf16[128,256]{1,0:T(8,128)(2,1)}), bf16[2048,256]{1,0:T(8,128)(2,1)}) %all-gather.16.cloned.1.call-update) | async-done | bytes 1048592 | tf_op jit(solution)/shard_map/all_gather | solution.py:158
  315.6 80.3 %all-gather.12.cloned.1.call-done = bf16[2048,2,256]{2,0,1:T(8,128)(2,1)} async-done(((bf16[128,2,256]{2,0,1:T(8,128)(2,1)}), bf16[2048,2,256]{2,0,1:T(8,128)(2,1)}) %all-gather.12.cloned.1.call-update) | async-done | bytes 2097168 | tf_op jit(solution)/shard_map/all_gather | solution.py:160
  395.9 79.9 %all-gather.14.cloned.1.call-done = bf16[2048,2,256]{2,0,1:T(8,128)(2,1)} async-done(((bf16[128,2,256]{2,0,1:T(8,128)(2,1)}), bf16[2048,2,256]{2,0,1:T(8,128)(2,1)}) %all-gather.14.cloned.1.call-update) | async-done | bytes 2097168 | tf_op jit(solution)/shard_map/all_gather | solution.py:161
  476.3 194.2 %while.29 = (s32[]{:T(128)}, f32[4,128]{1,0:T(4,128)S(1)}, f32[4,128]{1,0:T(4,128)}, f32[128,4,64]{0,2,1:T(8,128)}, f32[2,4,128]{2,0,1:T(2,128)S(1)}, /*index=5*...) while((s32[]{:T(128)}, f32[4,128]{1,0:T(4,128)S(1)}, ...), condition=%wide.region_7.8_spmd.clone, body=%wide.region_0.7_spmd.clone.sunk | while | flops 325065856 | bytes 26266780 | solution.py:173
  476.3 1.2 dynamic_slice.87
  479.9 1.6 constant_dynamic-slice_fusion.10
  484.9 1.2 convolution_bitcast_fusion.10
  486.1 1.5 multiply_convert_fusion.2
  488.6 1.4 convert_reduce_fusion.2
  491.5 1.7 fusion.155
  499.9 1.2 dynamic_slice.87
  503.5 1.6 constant_dynamic-slice_fusion.10
  509.7 1.5 multiply_convert_fusion.2
  512.3 1.4 convert_reduce_fusion.2
  513.6 1.2 fusion.146
  515.8 1.8 fusion.155
  524.3 1.2 dynamic_slice.87
  527.9 1.6 constant_dynamic-slice_fusion.10
  534.1 1.5 multiply_convert_fusion.2
  536.6 1.4 convert_reduce_fusion.2
  538.0 1.2 fusion.146
  540.2 1.8 fusion.155
  548.7 1.2 dynamic_slice.87
  552.2 1.6 constant_dynamic-slice_fusion.10
  558.5 1.5 multiply_convert_fusion.2
  561.0 1.4 convert_reduce_fusion.2
  562.4 1.2 fusion.146
  564.6 1.8 fusion.155
  573.1 1.2 dynamic_slice.87
  576.6 1.6 constant_dynamic-slice_fusion.10
  582.8 1.5 multiply_convert_fusion.2
  585.4 1.4 convert_reduce_fusion.2
  586.7 1.2 fusion.146
  589.0 1.8 fusion.155
  597.4 1.2 dynamic_slice.87
  601.0 1.6 constant_dynamic-slice_fusion.10
  607.2 1.5 multiply_convert_fusion.2
  609.7 1.4 convert_reduce_fusion.2
  611.1 1.2 fusion.146
  613.3 1.8 fusion.155
  621.8 1.2 dynamic_slice.87
  625.4 1.6 constant_dynamic-slice_fusion.10
  631.6 1.5 multiply_convert_fusion.2
  634.1 1.4 convert_reduce_fusion.2
  635.5 1.2 fusion.146
  637.7 1.8 fusion.155
  646.2 1.2 dynamic_slice.87
  649.7 1.6 constant_dynamic-slice_fusion.10
  655.9 1.5 multiply_convert_fusion.2
  658.5 1.4 convert_reduce_fusion.2
  659.9 1.2 fusion.146
  662.1 1.8 fusion.155
  672.4 1.8 add_convert_fusion
  674.2 1.2 fusion.36
  677.1 257.1 %all-reduce.2.cloned.1.call-done = bf16[128,256]{0,1:T(8,128)(2,1)} async-done(((bf16[128,256]{0,1:T(8,128)(2,1)}), bf16[128,256]{0,1:T(8,128)(2,1)}) %all-reduce.2.cloned.1.call-update) | async-done | bytes 65552 | tf_op jit(solution)/shard_map/psum | solution.py:188
  (453 shorter events, 131.7 us)
Async XLA Ops:
  7.2 11.3 %copy-start = (bf16[128,2048]{1,0:T(8,128)(2,1)S(1)}, bf16[128,2048]{1,0:T(8,128)(2,1)}, u32[]{:S(2)}) copy-start(bf16[128,2048]{1,0:T(8,128)(2,1)} %param.17) | copy-start | bytes 1572868
  7.2 10.3 %copy-start.5 = (bf16[256,256]{1,0:T(8,128)(2,1)S(1)}, bf16[256,256]{1,0:T(8,128)(2,1)}, u32[]{:S(2)}) copy-start(bf16[256,256]{1,0:T(8,128)(2,1)} %param.20) | copy-start | bytes 393220
  7.2 83.2 %all-gather.8.cloned.1.call-start = ((), (), s32[]{:S(2)}) async-start(), calls=%async_computation.1 | async-start | bytes 1114112 | tf_op jit(solution)/shard_map/all_gather | solution.py:156
  9.1 155.9 %all-gather.18.cloned.1.call-start = ((), (), s32[]{:S(2)}) async-start(), calls=%async_computation.6 | async-start | bytes 1114112 | tf_op jit(solution)/shard_map/all_gather | solution.py:159
  10.9 229.5 %all-gather.10.cloned.1.call-start = ((), (), s32[]{:S(2)}) async-start(), calls=%async_computation.2 | async-start | bytes 1114112 | tf_op jit(solution)/shard_map/all_gather | solution.py:157
  12.7 302.9 %all-gather.16.cloned.1.call-start = ((), (), s32[]{:S(2)}) async-start(), calls=%async_computation.5 | async-start | bytes 1114112 | tf_op jit(solution)/shard_map/all_gather | solution.py:158
  14.5 381.4 %all-gather.12.cloned.1.call-start = ((), (), s32[]{:S(2)}) async-start(), calls=%async_computation.3 | async-start | bytes 2228224 | tf_op jit(solution)/shard_map/all_gather | solution.py:160
  15.5 15.8 %copy-start.6 = (bf16[256,256]{1,0:T(8,128)(2,1)S(1)}, bf16[256,256]{1,0:T(8,128)(2,1)}, u32[]{:S(2)}) copy-start(bf16[256,256]{1,0:T(8,128)(2,1)} %param.18) | copy-start | bytes 393220
  17.4 15.1 %copy-start.18 = (s32[128]{0:T(128)S(1)}, s32[128]{0:T(128)}, u32[]{:S(2)}) copy-start(s32[128]{0:T(128)} %param.16) | copy-start | bytes 1540
  17.4 50.7 %copy-start.8 = (bf16[128,256]{1,0:T(8,128)(2,1)S(1)}, bf16[128,256]{1,0:T(8,128)(2,1)}, u32[]{:S(2)}) copy-start(bf16[128,256]{1,0:T(8,128)(2,1)} %param.13) | copy-start | bytes 196612
  17.4 458.3 %all-gather.14.cloned.1.call-start = ((), (), s32[]{:S(2)}) async-start(), calls=%async_computation.4 | async-start | bytes 2228224 | tf_op jit(solution)/shard_map/all_gather | solution.py:161
  17.8 51.2 %copy-start.10 = (bf16[128,256]{1,0:T(8,128)(2,1)S(1)}, bf16[128,256]{1,0:T(8,128)(2,1)}, u32[]{:S(2)}) copy-start(bf16[128,256]{1,0:T(8,128)(2,1)} %param.14) | copy-start | bytes 196612
  19.4 50.5 %all-to-all-start = ((bf16[128,16,128]{2,0,1:T(8,128)(2,1)}), bf16[128,16,128]{2,0,1:T(8,128)(2,1)}, u32[]{:S(2)}, u32[]{:S(2)}) async-start(bf16[128,16,128]{2,0,1:T(8,128)(2,1)} %copy_bitcast_fusion), calls=%async_computation | async-start | bytes 1048576 | tf_op jit(solution)/shard_map/all_to_all | solution.py:35
  31.2 902.9 %all-reduce.2.cloned.1.call-start = ((), (), s32[]{:S(2)}) async-start(), calls=%async_computation.7 | async-start | bytes 131072 | tf_op jit(solution)/shard_map/psum | solution.py:188
  476.3 5.2 copy-start.16
  490.0 6.7 copy-start.4
  494.4 3.5 copy-start.1
  496.7 2.3 copy-start.2
  497.9 2.1 copy-start.17
  499.9 5.2 copy-start.16
  513.6 7.5 copy-start.4
  518.8 3.5 copy-start.1
  521.1 2.3 copy-start.2
  522.2 1.4 copy-start.14
  522.2 2.1 copy-start.17
  524.3 5.2 copy-start.16
  538.0 7.5 copy-start.4
  543.1 3.5 copy-start.1
  545.5 2.3 copy-start.2
  546.6 1.5 copy-start.14
  546.6 2.1 copy-start.17
  548.7 5.2 copy-start.16
  562.4 7.5 copy-start.4
  567.5 3.5 copy-start.1
  569.8 2.3 copy-start.2
  571.0 1.5 copy-start.14
  571.0 2.1 copy-start.17
  573.1 5.2 copy-start.16
  586.7 7.5 copy-start.4
  591.9 3.5 copy-start.1
  594.2 2.3 copy-start.2
  595.3 1.5 copy-start.14
  595.3 2.1 copy-start.17
  597.4 5.2 copy-start.16
  611.1 7.5 copy-start.4
  616.2 3.5 copy-start.1
  618.6 2.3 copy-start.2
  619.7 1.5 copy-start.14
  619.7 2.1 copy-start.17
  621.8 5.2 copy-start.16
  635.5 7.5 copy-start.4
  640.6 3.5 copy-start.1
  642.9 2.3 copy-start.2
  644.1 1.5 copy-start.14
  644.1 2.1 copy-start.17
  646.2 5.2 copy-start.16
  659.8 7.5 copy-start.4
  665.0 3.5 copy-start.1
  667.3 2.3 copy-start.2
  668.5 1.5 copy-start.14
  668.5 2.1 copy-start.17
  670.5 4.9 copy-start.7
  670.5 4.9 copy-start.9
  670.5 264.5 %copy-start.11 = (bf16[128,256]{1,0:T(8,128)(2,1)S(1)}, bf16[128,256]{1,0:T(8,128)(2,1)}, u32[]{:S(2)}) copy-start(bf16[128,256]{1,0:T(8,128)(2,1)} %param.14) | copy-start | bytes 196612
  (33 other events, 27.7 us)
Sparse Core Ops, SparseCore 0:
  10.7 79.6 all-gather.7
  92.5 72.4 all-gather.17
  167.1 73.2 all-gather.9
  242.3 73.2 all-gather.15
  317.5 78.3 all-gather.11
  397.8 77.8 all-gather.13
  674.3 259.7 all-reduce.1
where the time goes:
time: 947 us; the launch traced here: 943 us
  waiting for transfers between devices  663 us (70%)
  matrix products  112 us (12%)
  local copies, waits for them, and re-layouts  65 us (7%)
  blocking collectives  34.9 us (4%)
  other arithmetic  34.7 us (4%)
  between operations  14.4 us (2%)
  starting transfers between devices  12.1 us (1%)
    psum x1, waiting for transfers between devices, on_device(): lax.psum(own_terms.reshape(rows, width).astype(jnp.bfloat16), 'tan')  257 us
    all_gather x1, waiting for transfers between devices, on_device(): lax.all_gather(own_tan_keys, 'blk', axis=0, tiled=True)  80.3 us
    all_gather x1, waiting for transfers between devices, on_device(): lax.all_gather(own_tan_values, 'blk', axis=0, tiled=True)  79.9 us
    all_gather x1, waiting for transfers between devices, on_device(): lax.all_gather(own_values, 'blk', axis=0, tiled=True)  75.4 us
    all_gather x1, waiting for transfers between devices, on_device(): lax.all_gather(own_lap_keys, 'blk', axis=0, tiled=True)  75.2 us
    all_gather x1, waiting for transfers between devices, on_device(): lax.all_gather(own_lap_values, 'blk', axis=0, tiled=True)  74.6 us
    dynamic_slice x80, local copies, waits for them, and re-layouts, on_device(): lax.scan(step, start_carry, (jnp.arange(parts, dtype=jnp.int32), stacked))  52.4 us
    all_gather x1, blocking collectives, on_device(): lax.all_gather(spin_wire, 'blk', axis=0, tiled=True)  34.9 us
  transfers between devices with their start and end apart: 8, of which 7 were waited for; matrix products, arithmetic and copies ran while one was open for 2% of the time, Pallas kernels for 0%

commit v1 on v0

--- a/solution.py
+++ b/solution.py
@@ -157,7 +157,9 @@
         lax.all_gather(own_values, "blk", axis=0, tiled=True),
         lax.all_gather(own_lap_keys, "blk", axis=0, tiled=True),
         lax.all_gather(own_lap_values, "blk", axis=0, tiled=True),
-        lax.all_gather(own_tan_keys, "blk", axis=0, tiled=True),
+        jnp.concatenate(
+            lax.all_to_all(jnp.stack([own_tan_keys] * lax.axis_size("blk")), "blk", 0, 0), axis=0
+        ),
         lax.all_gather(own_tan_values, "blk", axis=0, tiled=True),
         lax.all_gather(spin_wire, "blk", axis=0, tiled=True),
     )

time: 947 us -> 867 us (0.916)
  waiting for transfers between devices: 663 us -> 586 us
    all_gather x1 -> x0, waiting for transfers between devices: 80.3 us -> none  [on_device(): lax.all_gather(own_tan_keys, 'blk', axis=0, tiled=True)]
    all_to_all x0 -> x1, waiting for transfers between devices: none -> 53.8 us  [on_device(): lax.all_to_all(jnp.stack([own_tan_keys] * lax.axis_size('blk')), 'blk', 0...]
    all_gather x1, waiting for transfers between devices: 74.6 us -> 43.9 us  [on_device(): lax.all_gather(own_lap_values, 'blk', axis=0, tiled=True)]
    all_gather x1, waiting for transfers between devices: 20.5 us -> 0.01 us  [on_device(): lax.all_gather(own_keys, 'blk', axis=0, tiled=True)]
    all_to_all x0 -> x1, starting transfers between devices: none -> 11.9 us  [on_device(): lax.all_to_all(jnp.stack([own_tan_keys] * lax.axis_size('blk')), 'blk', 0...]
  transfers between devices with their start and end apart: 8 -> 8, of which waited for: 7 -> 6; matrix products, arithmetic and copies ran while one was open for 2% -> 2% of each run, Pallas kernels for 0% -> 0%
where the time goes in v1:
time: 867 us; the launch traced here: 863 us
  waiting for transfers between devices  586 us (68%)
  matrix products  111 us (13%)
  local copies, waits for them, and re-layouts  61.3 us (7%)
  blocking collectives  32.7 us (4%)
  other arithmetic  30 us (3%)
  starting transfers between devices  19.8 us (2%)
  between operations  14.4 us (2%)
    psum x1, waiting for transfers between devices, on_device(): lax.psum(own_terms.reshape(rows, width).astype(jnp.bfloat16), 'tan')  257 us
    all_gather x1, waiting for transfers between devices, on_device(): lax.all_gather(own_tan_values, 'blk', axis=0, tiled=True)  80.3 us
    all_gather x1, waiting for transfers between devices, on_device(): lax.all_gather(own_lap_keys, 'blk', axis=0, tiled=True)  75.2 us
    all_gather x1, waiting for transfers between devices, on_device(): lax.all_gather(own_values, 'blk', axis=0, tiled=True)  75.2 us
    all_to_all x1, waiting for transfers between devices, on_device(): lax.all_to_all(jnp.stack([own_tan_keys] * lax.axis_size('blk')), 'blk', 0...  53.8 us
    dynamic_slice x80, local copies, waits for them, and re-layouts, on_device(): lax.scan(step, start_carry, (jnp.arange(parts, dtype=jnp.int32), stacked))  47.3 us
    all_gather x1, waiting for transfers between devices, on_device(): lax.all_gather(own_lap_values, 'blk', axis=0, tiled=True)  43.9 us
    all_gather x1, blocking collectives, on_device(): lax.all_gather(spin_wire, 'blk', axis=0, tiled=True)  32.7 us
  transfers between devices with their start and end apart: 8, of which 6 were waited for; matrix products, arithmetic and copies ran while one was open for 2% of the time, Pallas kernels for 0%

profile of v1, /device:TPU:8, one launch (start us, length us, event | category | flops | bytes accessed | tf_op | source)
XLA Modules:
  0.0 863.1 jit_solution(13705068613016763588)
XLA Ops:
  7.2 1.8 convolution_convert_fusion.8
  9.1 1.7 convolution_convert_fusion.3
  10.9 1.7 convolution_convert_fusion.6
  12.7 1.7 convolution_convert_fusion.4
  16.6 1.6 stack.3
  18.2 11.9 %all-to-all-start.1 = ((bf16[16,128,2,256]{3,1,2,0:T(8,128)(2,1)}), bf16[16,128,2,256]{3,1,2,0:T(8,128)(2,1)S(1)}, u32[]{:S(2)}, u32[]{:S(2)}) async-start(bf16[16,128,2,256]{3,1,2,0:T(8,128)(2,1)} %stack.3), calls=%async_computation.1 | async-start | bytes 4194304 | tf_op jit(solution)/shard_map/all_to_all | solution.py:161
  32.1 53.8 %all-to-all-done.1 = bf16[16,128,2,256]{3,1,2,0:T(8,128)(2,1)S(1)} async-done(((bf16[16,128,2,256]{3,1,2,0:T(8,128)(2,1)}), bf16[16,128,2,256]{3,1,2,0:T(8,128)(2,1)S(1)}, u32[]{:S(2)}, u32[]{:S(2)}) %all-to-all-start.1) | async-done | bytes 2097184 | tf_op jit(solution)/shard_map/all_to_all | solution.py:161
  85.9 7.6 all-to-all-start
  94.8 32.7 %all-gather = bf16[16,1,128]{2,1,0:T(2,128)(2,1)S(1)} all-gather(bf16[1,1,128]{2,1,0:T(2,128)(2,1)S(1)} %get-tuple-element.593), channel_id=1, replica_groups=mesh['blk'=16,'tan'=32] {'blk'}, dimensions={0}, use_global_device_ids=true | all-gather | bytes 4352 | tf_op jit(solution)/shard_map/all_gather | solution.py:164
  129.4 1.5 copy.99
  130.8 43.9 %all-gather.15.cloned.1.call-done = bf16[2048,256]{1,0:T(8,128)(2,1)} async-done(((bf16[128,256]{1,0:T(8,128)(2,1)}), bf16[2048,256]{1,0:T(8,128)(2,1)}) %all-gather.15.cloned.1.call-update) | async-done | bytes 1048592 | tf_op jit(solution)/shard_map/all_gather | solution.py:159
  174.7 75.2 %all-gather.9.cloned.1.call-done = bf16[2048,256]{1,0:T(8,128)(2,1)} async-done(((bf16[128,256]{1,0:T(8,128)(2,1)}), bf16[2048,256]{1,0:T(8,128)(2,1)}) %all-gather.9.cloned.1.call-update) | async-done | bytes 1048592 | tf_op jit(solution)/shard_map/all_gather | solution.py:157
  249.9 75.2 %all-gather.13.cloned.1.call-done = bf16[2048,256]{1,0:T(8,128)(2,1)} async-done(((bf16[128,256]{1,0:T(8,128)(2,1)}), bf16[2048,256]{1,0:T(8,128)(2,1)}) %all-gather.13.cloned.1.call-update) | async-done | bytes 1048592 | tf_op jit(solution)/shard_map/all_gather | solution.py:158
  325.1 80.3 %all-gather.11.cloned.1.call-done = bf16[2048,2,256]{2,0,1:T(8,128)(2,1)} async-done(((bf16[128,2,256]{2,0,1:T(8,128)(2,1)}), bf16[2048,2,256]{2,0,1:T(8,128)(2,1)}) %all-gather.11.cloned.1.call-update) | async-done | bytes 2097168 | tf_op jit(solution)/shard_map/all_gather | solution.py:163
  405.5 185.5 %while.29 = (s32[]{:T(128)}, f32[4,128]{1,0:T(4,128)S(1)}, f32[4,128]{1,0:T(4,128)}, f32[128,4,64]{0,2,1:T(8,128)}, f32[2,4,128]{2,0,1:T(2,128)S(1)}, /*index=5*...) while((s32[]{:T(128)}, f32[4,128]{1,0:T(4,128)S(1)}, ...), condition=%wide.region_7.8_spmd.clone, body=%wide.region_0.7_spmd.clone.sunk | while | flops 325065856 | bytes 26300116 | solution.py:175
  407.8 1.6 constant_dynamic-slice_fusion.10
  412.8 1.2 convolution_bitcast_fusion.10
  414.0 1.5 multiply_convert_fusion.2
  416.5 1.4 convert_reduce_fusion.2
  419.5 1.7 fusion.155
  430.3 1.6 constant_dynamic-slice_fusion.10
  435.3 1.2 convolution_bitcast_fusion.10
  436.5 1.5 multiply_convert_fusion.2
  439.0 1.4 convert_reduce_fusion.2
  440.4 1.3 fusion.146
  442.7 1.8 fusion.155
  453.6 1.6 constant_dynamic-slice_fusion.10
  458.6 1.2 convolution_bitcast_fusion.10
  459.7 1.5 multiply_convert_fusion.2
  462.3 1.4 convert_reduce_fusion.2
  463.7 1.3 fusion.146
  466.0 1.8 fusion.155
  476.8 1.6 constant_dynamic-slice_fusion.10
  481.8 1.2 convolution_bitcast_fusion.10
  483.0 1.5 multiply_convert_fusion.2
  485.6 1.4 convert_reduce_fusion.2
  487.0 1.3 fusion.146
  489.3 1.8 fusion.155
  500.1 1.6 constant_dynamic-slice_fusion.10
  505.1 1.2 convolution_bitcast_fusion.10
  506.3 1.5 multiply_convert_fusion.2
  508.9 1.4 convert_reduce_fusion.2
  510.2 1.3 fusion.146
  512.6 1.8 fusion.155
  523.4 1.6 constant_dynamic-slice_fusion.10
  528.4 1.2 convolution_bitcast_fusion.10
  529.6 1.5 multiply_convert_fusion.2
  532.1 1.4 convert_reduce_fusion.2
  533.5 1.3 fusion.146
  535.9 1.8 fusion.155
  546.7 1.6 constant_dynamic-slice_fusion.10
  551.7 1.2 convolution_bitcast_fusion.10
  552.9 1.5 multiply_convert_fusion.2
  555.4 1.4 convert_reduce_fusion.2
  556.8 1.3 fusion.146
  559.1 1.8 fusion.155
  570.0 1.6 constant_dynamic-slice_fusion.10
  576.2 1.5 multiply_convert_fusion.2
  578.7 1.4 convert_reduce_fusion.2
  580.1 1.3 fusion.146
  582.4 1.8 fusion.155
  592.9 1.8 add_convert_fusion
  594.6 1.2 fusion.36
  597.5 257.0 %all-reduce.2.cloned.1.call-done = bf16[128,256]{0,1:T(8,128)(2,1)} async-done(((bf16[128,256]{0,1:T(8,128)(2,1)}), bf16[128,256]{0,1:T(8,128)(2,1)}) %all-reduce.2.cloned.1.call-update) | async-done | bytes 65552 | tf_op jit(solution)/shard_map/psum | solution.py:190
  (554 shorter events, 122.0 us)
Async XLA Ops:
  7.2 24.0 %copy-start = (bf16[128,2048]{1,0:T(8,128)(2,1)S(1)}, bf16[128,2048]{1,0:T(8,128)(2,1)}, u32[]{:S(2)}) copy-start(bf16[128,2048]{1,0:T(8,128)(2,1)} %param.17) | copy-start | bytes 1572868
  7.2 123.7 %all-gather.7.cloned.1.call-start = ((), (), s32[]{:S(2)}) async-start(), calls=%async_computation.2 | async-start | bytes 1114112 | tf_op jit(solution)/shard_map/all_gather | solution.py:156
  9.0 165.7 %all-gather.15.cloned.1.call-start = ((), (), s32[]{:S(2)}) async-start(), calls=%async_computation.6 | async-start | bytes 1114112 | tf_op jit(solution)/shard_map/all_gather | solution.py:159
  10.8 239.1 %all-gather.9.cloned.1.call-start = ((), (), s32[]{:S(2)}) async-start(), calls=%async_computation.3 | async-start | bytes 1114112 | tf_op jit(solution)/shard_map/all_gather | solution.py:157
  12.6 312.5 %all-gather.13.cloned.1.call-start = ((), (), s32[]{:S(2)}) async-start(), calls=%async_computation.5 | async-start | bytes 1114112 | tf_op jit(solution)/shard_map/all_gather | solution.py:158
  18.2 12.0 %copy-start.5 = (bf16[256,256]{1,0:T(8,128)(2,1)S(1)}, bf16[256,256]{1,0:T(8,128)(2,1)}, u32[]{:S(2)}) copy-start(bf16[256,256]{1,0:T(8,128)(2,1)} %param.20) | copy-start | bytes 393220
  18.2 67.7 %all-to-all-start.1 = ((bf16[16,128,2,256]{3,1,2,0:T(8,128)(2,1)}), bf16[16,128,2,256]{3,1,2,0:T(8,128)(2,1)S(1)}, u32[]{:S(2)}, u32[]{:S(2)}) async-start(bf16[16,128,2,256]{3,1,2,0:T(8,128)(2,1)} %stack.3), calls=%async_computation.1 | async-start | bytes 4194304 | tf_op jit(solution)/shard_map/all_to_all | solution.py:161
  30.1 63.5 %copy-start.6 = (bf16[256,256]{1,0:T(8,128)(2,1)S(1)}, bf16[256,256]{1,0:T(8,128)(2,1)}, u32[]{:S(2)}) copy-start(bf16[256,256]{1,0:T(8,128)(2,1)} %param.18) | copy-start | bytes 393220
  30.1 64.7 %copy-start.24 = (s32[128]{0:T(128)S(1)}, s32[128]{0:T(128)}, u32[]{:S(2)}) copy-start(s32[128]{0:T(128)} %param.16) | copy-start | bytes 1540
  30.1 97.5 %copy-start.8 = (bf16[128,256]{1,0:T(8,128)(2,1)S(1)}, bf16[128,256]{1,0:T(8,128)(2,1)}, u32[]{:S(2)}) copy-start(bf16[128,256]{1,0:T(8,128)(2,1)} %param.13) | copy-start | bytes 196612
  30.1 375.3 %all-gather.11.cloned.1.call-start = ((), (), s32[]{:S(2)}) async-start(), calls=%async_computation.4 | async-start | bytes 2228224 | tf_op jit(solution)/shard_map/all_gather | solution.py:163
  30.4 98.0 %copy-start.10 = (bf16[128,256]{1,0:T(8,128)(2,1)S(1)}, bf16[128,256]{1,0:T(8,128)(2,1)}, u32[]{:S(2)}) copy-start(bf16[128,256]{1,0:T(8,128)(2,1)} %param.14) | copy-start | bytes 196612
  85.9 44.9 %all-to-all-start = ((bf16[128,16,128]{2,0,1:T(8,128)(2,1)}), bf16[128,16,128]{2,0,1:T(8,128)(2,1)}, u32[]{:S(2)}, u32[]{:S(2)}) async-start(bf16[128,16,128]{2,0,1:T(8,128)(2,1)} %copy_bitcast_fusion), calls=%async_computation | async-start | bytes 1048576 | tf_op jit(solution)/shard_map/all_to_all | solution.py:35
  93.5 761.0 %all-reduce.2.cloned.1.call-start = ((), (), s32[]{:S(2)}) async-start(), calls=%async_computation.7 | async-start | bytes 131072 | tf_op jit(solution)/shard_map/psum | solution.py:190
  129.4 276.1 %copy-start.18 = (f32[4]{0:T(128)S(1)}, f32[4]{0:T(128)}, u32[]{:S(2)}) copy-start(f32[4]{0:T(128)} %param.22) | copy-start | bytes 52
  129.4 276.1 %copy-start.20 = (f32[4]{0:T(128)S(1)}, f32[4]{0:T(128)}, u32[]{:S(2)}) copy-start(f32[4]{0:T(128)} %param.23) | copy-start | bytes 52
  405.5 7.1 copy-start.16
  405.5 7.1 copy-start.22
  417.9 6.8 copy-start.4
  422.4 3.5 copy-start.1
  424.7 2.4 copy-start.2
  428.0 2.2 copy-start.25
  428.0 7.1 copy-start.16
  428.0 7.1 copy-start.22
  440.4 7.6 copy-start.4
  445.6 3.5 copy-start.1
  448.0 2.4 copy-start.2
  451.2 2.2 copy-start.25
  451.3 7.1 copy-start.16
  451.3 7.1 copy-start.22
  463.7 7.6 copy-start.4
  468.9 3.5 copy-start.1
  471.2 2.4 copy-start.2
  474.5 2.2 copy-start.25
  474.5 7.1 copy-start.16
  474.6 7.1 copy-start.22
  486.9 7.6 copy-start.4
  492.2 3.5 copy-start.1
  494.5 2.4 copy-start.2
  497.8 2.2 copy-start.25
  497.8 7.1 copy-start.16
  497.8 7.1 copy-start.22
  510.2 7.6 copy-start.4
  515.5 3.5 copy-start.1
  517.8 2.4 copy-start.2
  521.1 7.1 copy-start.16
  521.1 7.1 copy-start.22
  533.5 7.6 copy-start.4
  538.8 3.5 copy-start.1
  541.1 2.4 copy-start.2
  544.4 2.2 copy-start.25
  544.4 7.1 copy-start.16
  544.4 7.1 copy-start.22
  556.8 7.6 copy-start.4
  562.1 3.5 copy-start.1
  564.4 2.4 copy-start.2
  567.7 7.1 copy-start.16
  567.7 7.1 copy-start.22
  580.1 7.6 copy-start.4
  585.3 3.5 copy-start.1
  587.7 2.4 copy-start.2
  590.9 4.9 copy-start.7
  591.0 4.9 copy-start.9
  591.0 264.4 %copy-start.11 = (bf16[128,256]{1,0:T(8,128)(2,1)S(1)}, bf16[128,256]{1,0:T(8,128)(2,1)}, u32[]{:S(2)}) copy-start(bf16[128,256]{1,0:T(8,128)(2,1)} %param.14) | copy-start | bytes 196612
  (83 other events, 128.5 us)
Sparse Core Ops, SparseCore 0:
  10.6 89.0 all-gather.6
  101.8 72.8 all-gather.14
  176.8 73.0 all-gather.8
  251.8 73.2 all-gather.12
  327.0 78.3 all-gather.10
  594.8 259.7 all-reduce.1
